TPU v7x, 32 devices: a whole 2x2x4 slice. The times are simulated.
32 devices in a mesh: frames: 2 (over x), date: 8 (over z, y), row: 2 (over core).
Axes of the slice: x: 2, y: 2, z: 4, core: 2. Of those that a mesh axis runs over, the one named last changes fastest.
Arguments:
- intensity: float32 [128, 512, 512], P(('frames', 'date'), 'row'), parts along dimension 0, may hold values from 0.05 to 20
Outputs:
- filtered: float32 [128, 512, 512], P(('frames', 'date'), 'row'), parts along dimension 0
- change: float32 [128, 512, 512], P(('frames', 'date'), 'row'), parts along dimension 0
There are 2 independent parts, one for each index of `frames`. A program takes and returns all parts, laid end to end along the dimension named above; each array names one. Nothing has to cross between parts.
All inputs are finite; a program needn't handle non-finite values.
Results may differ from a plain program's by a relative error of at most 0.00002.
Values sent between devices are 32-bit elements; how exact they have to be, the bound alone decides.
A program may use at most 64 MiB of HBM per device.

v0:
```python
import jax
import jax.numpy as jnp
from jax import lax
from jax.sharding import PartitionSpec as P

RADIUS = 3


def padded_2(cells, sides, width):
    for axis, dim in sides:
        count = lax.axis_size(axis)
        ends = count - 1
        head = lax.slice_in_dim(cells, 0, width, axis=dim)
        tail = lax.slice_in_dim(cells, cells.shape[dim] - width, cells.shape[dim], axis=dim)
        cells = jnp.concatenate(
            [
                lax.ppermute(tail, axis, [(i, (i + 1) % count) for i in range(ends)]),
                cells,
                lax.ppermute(head, axis, [((i + 1) % count, i) for i in range(ends)]),
            ],
            axis=dim,
        )
    return cells


def shifted(block, axis, distance):
    devices = range(lax.axis_size(axis))
    route = [(i - distance, i) for i in devices if i - distance in devices]
    return lax.ppermute(block, axis, route)


def rim_sum(haloed, rows_n):
    width = 2 * RADIUS + 1
    cols_n = haloed.shape[2]
    padded = jnp.pad(haloed, ((0, 0), (0, 0), (RADIUS, RADIUS)))
    across = padded[:, 0:rows_n, :]
    for offset in range(1, width):
        across = across + padded[:, offset : offset + rows_n, :]
    total = across[:, :, 0:cols_n]
    for offset in range(1, width):
        total = total + across[:, :, offset : offset + cols_n]
    return total


def valid_count(first, length, extent):
    places = first + jnp.arange(length, dtype=jnp.int32)
    counted = jnp.zeros((length,), jnp.float32)
    for offset in range(-RADIUS, RADIUS + 1):
        inside = (places + offset >= 0) & (places + offset < extent)
        counted = counted + inside.astype(jnp.float32)
    return counted


def on_device(intensity):
    rows_n = intensity.shape[1]
    cols_n = intensity.shape[2]
    row_groups = lax.axis_size("row")
    date_groups = lax.axis_size("date")
    total_dates = intensity.shape[0] * date_groups
    row_first = lax.axis_index("row") * rows_n
    row_count = valid_count(row_first, rows_n, rows_n * row_groups)
    col_count = valid_count(jnp.int32(0), cols_n, cols_n)
    count = row_count[:, None] * col_count[None, :]
    haloed = padded_2(intensity, (("row", 1),), RADIUS)
    local_mean = rim_sum(haloed, rows_n) / count[None]
    is_last = lax.axis_index("date") == date_groups - 1
    ratio_sum = lax.psum(jnp.sum(intensity / local_mean, axis=0), "date")
    scale = ratio_sum[None] / jnp.float32(total_dates)
    filtered = local_mean * scale
    following = shifted(haloed[0:1], "date", -1)
    follow_mean = rim_sum(following, rows_n) / count[None]
    successor = jnp.where(is_last, filtered[-1:], follow_mean * scale)
    logged = jnp.log(filtered)
    ahead = jnp.concatenate([logged[1:], jnp.log(successor)], axis=0)
    change = ahead - logged
    return (filtered, change)


def solution(mesh):
    return jax.shard_map(
        on_device,
        mesh=mesh,
        in_specs=(P(("frames", "date"), "row", None),),
        out_specs=(P(("frames", "date"), "row", None), P(("frames", "date"), "row", None)),
        check_vma=False,
    )
```

profile of v0, /device:TPU:0, one launch (start us, length us, event | category | flops | bytes accessed | tf_op | source)
XLA Modules:
  0.0 132.5 jit_solution(6093644278905989527)
XLA Ops:
  7.2 0.0 all-reduce.4.cloned.1.call-start
  7.2 1.0 fusion.42
  8.2 2.4 %collective-permute-start = (f32[8,3,512]{2,1,0:T(4,128)S(1)}, f32[8,3,512]{2,1,0:T(4,128)S(1)}, u32[]{:S(2)}, u32[]{:S(2)}) collective-permute-start(f32[8,3,512]{2,1,0:T(4,128)S(1)} %get-tuple-element.6), channel_id=1, source_target_pairs={{0,1},{2,3},{4,5},{6,7},{8,9},{10,11},{12,13},{14,15},{16,17},{18,... | collective-permute-start | bytes 147464 | tf_op jit(solution)/shard_map/ppermute | solution.py:17
  10.6 1.3 collective-permute-start.1
  12.0 0.1 broadcast_multiply_fusion.1
  12.1 0.0 collective-permute-done
  12.1 1.7 %collective-permute-done.1 = f32[8,3,512]{2,1,0:T(4,128)S(1)} collective-permute-done((f32[8,3,512]{2,1,0:T(4,128)S(1)}, f32[8,3,512]{2,1,0:T(4,128)S(1)}, u32[]{:S(2)}, u32[]{:S(2)}) %collective-permute-start.1) | collective-permute-done | bytes 49184 | tf_op jit(solution)/shard_map/ppermute | solution.py:19
  13.8 2.8 %pad_maximum_fusion = f32[8,262,512]{2,1,0:T(8,128)S(1)} fusion(f32[8,3,512]{2,1,0:T(4,128)S(1)} %collective-permute-done.1, f32[8,256,512]{2,1,0:T(8,128)} %param.1, f32[8,3,512]{2,1,0:T(4,128)S(1)} %collective-permute-done), kind=kLoop, calls=%fused_computation.13 | loop fusion | flops 2146304 | bytes 8585216 | tf_op jit(solution)/shard_map/concatenate | solution.py:15
  16.5 11.3 %fusion.5 = f32[8,256,518]{2,1,0:T(8,128)S(1)} fusion(f32[8,262,512]{2,1,0:T(8,128)S(1)} %pad_maximum_fusion), kind=kLoop, calls=%fused_computation.12 | loop fusion | flops 6365184 | bytes 8536064 | tf_op jit(solution)/shard_map/add | solution.py:38
  27.9 10.4 %fusion.6 = (f32[256,512]{1,0:T(8,128)}, f32[8,256,512]{2,1,0:T(8,128)}) fusion(f32[8,256,512]{2,1,0:T(8,128)} %param.1, f32[256,512]{1,0:T(8,128)S(1)} %broadcast_multiply_fusion.1, f32[8,256,518]{2,1,0:T(8,128)S(1)} %fusion.5), kind=kLoop, calls=%fused_computation.23 | loop fusion | flops 9306112 | bytes 38797312 | tf_op jit(solution)/shard_map/reduce_sum | solution.py:67
  38.3 0.0 all-reduce.4.cloned.1.call-update
  38.3 1.1 slice.141
  39.4 1.5 %collective-permute-start.2 = (f32[1,262,512]{2,1,0:T(8,128)S(1)}, f32[1,262,512]{2,1,0:T(8,128)S(1)}, u32[]{:S(2)}, u32[]{:S(2)}) collective-permute-start(f32[1,262,512]{2,1,0:T(8,128)S(1)} %slice.141), channel_id=1, source_target_pairs={{2,0},{4,2},{6,4},{8,6},{10,8},{12,10},{14,12},{3,1},{5,3},{7,5},{... | collective-permute-start | bytes 1609736 | tf_op jit(solution)/shard_map/ppermute | solution.py:29
  40.9 74.4 %all-reduce.4.cloned.1.call-done = f32[256,512]{1,0:T(8,128)} async-done(((f32[256,512]{1,0:T(8,128)}), f32[256,512]{1,0:T(8,128)}) %all-reduce.4.cloned.1.call-update) | async-done | bytes 524304 | tf_op jit(solution)/shard_map/psum | solution.py:67
  115.3 1.1 broadcast_multiply_fusion
  116.4 3.3 %fusion.41 = (f32[8,256,512]{2,1,0:T(8,128)S(1)}, f32[8,256,512]{2,1,0:T(8,128)S(1)}) fusion(f32[256,512]{1,0:T(8,128)S(1)} %broadcast_multiply_fusion, f32[8,256,512]{2,1,0:T(8,128)} %get-tuple-element.5, f32[256,512]{1,0:T(8,128)S(1)} %broadcast_multiply_fusion.1), kind=kLoop, calls=%fused_computation.88 | loop fusion | flops 2097152 | bytes 13631488 | tf_op jit(solution)/shard_map/log | solution.py:73
  119.7 0.0 copy-start.1
  119.7 0.0 copy-start.2
  119.7 0.5 slice.139
  120.3 0.0 collective-permute-done.2
  120.3 1.4 %fusion.12 = f32[1,256,518]{2,1,0:T(8,128)S(1)} fusion(f32[1,262,512]{2,1,0:T(8,128)S(1)} %collective-permute-done.2), kind=kLoop, calls=%fused_computation.36 | loop fusion | flops 795648 | bytes 1067008 | tf_op jit(solution)/shard_map/add | solution.py:38
  121.7 0.0 copy-done.2
  121.7 0.9 fusion.16
  122.6 3.0 %maximum_subtract_fusion = f32[8,256,512]{2,1,0:T(8,128)} fusion(f32[1,256,512]{2,1,0:T(8,128)S(1)} %fusion.16, f32[7,256,512]{2,1,0:T(8,128)S(1)} %slice.139, f32[8,256,512]{2,1,0:T(8,128)S(1)} %get-tuple-element.3), kind=kLoop, calls=%fused_computation.20 | loop fusion | flops 2097152 | bytes 12582912 | tf_op jit(solution)/shard_map/sub | solution.py:75
  (5 shorter events, 0.0 us)
Async XLA Ops:
  7.2 108.1 %all-reduce.4.cloned.1.call-start = ((), (), s32[]{:S(2)}) async-start(), calls=%async_computation | async-start | bytes 1048576 | tf_op jit(solution)/shard_map/psum | solution.py:67
  8.2 3.9 %collective-permute-start = (f32[8,3,512]{2,1,0:T(4,128)S(1)}, f32[8,3,512]{2,1,0:T(4,128)S(1)}, u32[]{:S(2)}, u32[]{:S(2)}) collective-permute-start(f32[8,3,512]{2,1,0:T(4,128)S(1)} %get-tuple-element.6), channel_id=1, source_target_pairs={{0,1},{2,3},{4,5},{6,7},{8,9},{10,11},{12,13},{14,15},{16,17},{18,... | collective-permute-start | bytes 147464 | tf_op jit(solution)/shard_map/ppermute | solution.py:17
  10.6 3.1 %collective-permute-start.1 = (f32[8,3,512]{2,1,0:T(4,128)S(1)}, f32[8,3,512]{2,1,0:T(4,128)S(1)}, u32[]{:S(2)}, u32[]{:S(2)}) collective-permute-start(f32[8,3,512]{2,1,0:T(4,128)S(1)} %get-tuple-element.7), channel_id=1, source_target_pairs={{1,0},{3,2},{5,4},{7,6},{9,8},{11,10},{13,12},{15,14},{17,16},{19,... | collective-permute-start | bytes 147464 | tf_op jit(solution)/shard_map/ppermute | solution.py:19
  16.5 11.3 %copy-start = (f32[8,262,512]{2,1,0:T(8,128)}, f32[8,262,512]{2,1,0:T(8,128)S(1)}, u32[]{:S(2)}) copy-start(f32[8,262,512]{2,1,0:T(8,128)S(1)} %pad_maximum_fusion) | copy-start | bytes 12877828
  39.4 80.9 %collective-permute-start.2 = (f32[1,262,512]{2,1,0:T(8,128)S(1)}, f32[1,262,512]{2,1,0:T(8,128)S(1)}, u32[]{:S(2)}, u32[]{:S(2)}) collective-permute-start(f32[1,262,512]{2,1,0:T(8,128)S(1)} %slice.141), channel_id=1, source_target_pairs={{2,0},{4,2},{6,4},{8,6},{10,8},{12,10},{14,12},{3,1},{5,3},{7,5},{... | collective-permute-start | bytes 1609736 | tf_op jit(solution)/shard_map/ppermute | solution.py:29
  119.7 3.0 %copy-start.1 = (f32[8,256,512]{2,1,0:T(8,128)}, f32[8,256,512]{2,1,0:T(8,128)S(1)}, u32[]{:S(2)}) copy-start(f32[8,256,512]{2,1,0:T(8,128)S(1)} %get-tuple-element.3) | copy-start | bytes 12582916
  119.7 2.0 %copy-start.2 = (f32[256,512]{1,0:T(8,128)S(1)}, f32[256,512]{1,0:T(8,128)}, u32[]{:S(2)}) copy-start(f32[256,512]{1,0:T(8,128)} %all-reduce.4.cloned.1.call-done) | copy-start | bytes 1572868
Sparse Core Ops, SparseCore 0:
  38.4 76.8 all-reduce.3
where the time goes:
time: 133 us
  waiting for transfers between devices  76.1 us (57%)
  other arithmetic  34.4 us (26%)
  between operations  14.2 us (11%)
  starting transfers between devices  5.2 us (4%)
  local copies, waits for them, and re-layouts  2.64 us (2%)
    psum x1, waiting for transfers between devices, on_device(): ratio_sum = lax.psum(jnp.sum(intensity / local_mean, axis=0), 'date')  74.4 us
    add x2, other arithmetic, rim_sum(): across = across + padded[:, offset:offset + rows_n, :]  12.7 us
    reduce_sum x1, other arithmetic, on_device(): ratio_sum = lax.psum(jnp.sum(intensity / local_mean, axis=0), 'date')  10.4 us
    log x1, other arithmetic, on_device(): logged = jnp.log(filtered)  3.32 us
    sub x1, other arithmetic, on_device(): change = ahead - logged  3.05 us
    concatenate x1, other arithmetic, padded_2(): jnp.concatenate([lax.ppermute(tail, axis, [(i, (i + 1) % count) for i in...  2.75 us
  transfers between devices with their start and end apart: 4, of which 2 were waited for; matrix products, arithmetic and copies ran while one was open for 5% of the time, Pallas kernels for 0%

commit v1 on v0

--- a/solution.py
+++ b/solution.py
@@ -64,7 +64,9 @@
     haloed = padded_2(intensity, (("row", 1),), RADIUS)
     local_mean = rim_sum(haloed, rows_n) / count[None]
     is_last = lax.axis_index("date") == date_groups - 1
-    ratio_sum = lax.psum(jnp.sum(intensity / local_mean, axis=0), "date")
+    block_2 = jnp.sum(intensity / local_mean, axis=0)
+    parts = lax.all_gather(block_2, "date")
+    ratio_sum = jnp.sum(parts, axis=0)
     scale = ratio_sum[None] / jnp.float32(total_dates)
     filtered = local_mean * scale
     following = shifted(haloed[0:1], "date", -1)

time: 133 us -> 137 us (1.030)
  waiting for transfers between devices: 76.1 us -> 77.7 us
  other arithmetic: 34.4 us -> 36 us
    psum x1 -> x0, waiting for transfers between devices: 74.4 us -> none  [on_device(): ratio_sum = lax.psum(jnp.sum(intensity / local_mean, axis=0), 'date')]
    all_gather x0 -> x1, waiting for transfers between devices: none -> 55.1 us  [on_device(): parts = lax.all_gather(block_2, 'date')]
    ppermute x1, waiting for transfers between devices: 0.01 us -> 20.9 us  [shifted(): return lax.ppermute(block, axis, route)]
    reduce_sum x1 -> x2, other arithmetic: 10.4 us -> 13.1 us  [the longest x1 10.4 us: on_device(): block_2 = jnp.sum(intensity / local_mean, axis=0)]
  transfers between devices with their start and end apart: 4 -> 4, of which waited for: 2 -> 3; matrix products, arithmetic and copies ran while one was open for 5% -> 2% of each run, Pallas kernels for 0% -> 0%
where the time goes in v1:
time: 137 us
  waiting for transfers between devices  77.7 us (57%)
  other arithmetic  36 us (26%)
  between operations  14.2 us (10%)
  starting transfers between devices  5.2 us (4%)
  local copies, waits for them, and re-layouts  3.75 us (3%)
    all_gather x1, waiting for transfers between devices, on_device(): parts = lax.all_gather(block_2, 'date')  55.1 us
    ppermute x1, waiting for transfers between devices, shifted(): return lax.ppermute(block, axis, route)  20.9 us
    add x2, other arithmetic, rim_sum(): across = across + padded[:, offset:offset + rows_n, :]  12.7 us
    reduce_sum x1, other arithmetic, on_device(): block_2 = jnp.sum(intensity / local_mean, axis=0)  10.4 us
    log x1, other arithmetic, on_device(): logged = jnp.log(filtered)  3.32 us
    sub x1, other arithmetic, on_device(): change = ahead - logged  3.04 us
    concatenate x1, other arithmetic, padded_2(): jnp.concatenate([lax.ppermute(tail, axis, [(i, (i + 1) % count) for i in...  2.75 us
  transfers between devices with their start and end apart: 4, of which 3 were waited for; matrix products, arithmetic and copies ran while one was open for 2% of the time, Pallas kernels for 0%

profile of v1, /device:TPU:0, one launch (start us, length us, event | category | flops | bytes accessed | tf_op | source)
XLA Modules:
  0.0 136.9 jit_solution(7975592479261989748)
XLA Ops:
  7.2 0.0 all-gather.3.cloned.1.call-start
  7.2 1.0 fusion.42
  8.2 2.4 %collective-permute-start = (f32[8,3,512]{2,1,0:T(4,128)S(1)}, f32[8,3,512]{2,1,0:T(4,128)S(1)}, u32[]{:S(2)}, u32[]{:S(2)}) collective-permute-start(f32[8,3,512]{2,1,0:T(4,128)S(1)} %get-tuple-element.6), channel_id=1, source_target_pairs={{0,1},{2,3},{4,5},{6,7},{8,9},{10,11},{12,13},{14,15},{16,17},{18,... | collective-permute-start | bytes 147464 | tf_op jit(solution)/shard_map/ppermute | solution.py:17
  10.6 1.3 collective-permute-start.1
  12.0 0.1 broadcast_multiply_fusion.1
  12.1 0.0 collective-permute-done
  12.1 1.7 %collective-permute-done.1 = f32[8,3,512]{2,1,0:T(4,128)S(1)} collective-permute-done((f32[8,3,512]{2,1,0:T(4,128)S(1)}, f32[8,3,512]{2,1,0:T(4,128)S(1)}, u32[]{:S(2)}, u32[]{:S(2)}) %collective-permute-start.1) | collective-permute-done | bytes 49184 | tf_op jit(solution)/shard_map/ppermute | solution.py:19
  13.8 2.8 %pad_maximum_fusion = f32[8,262,512]{2,1,0:T(8,128)S(1)} fusion(f32[8,3,512]{2,1,0:T(4,128)S(1)} %collective-permute-done.1, f32[8,256,512]{2,1,0:T(8,128)} %param.1, f32[8,3,512]{2,1,0:T(4,128)S(1)} %collective-permute-done), kind=kLoop, calls=%fused_computation.13 | loop fusion | flops 2146304 | bytes 8585216 | tf_op jit(solution)/shard_map/concatenate | solution.py:15
  16.5 11.3 %fusion.5 = f32[8,256,518]{2,1,0:T(8,128)S(1)} fusion(f32[8,262,512]{2,1,0:T(8,128)S(1)} %pad_maximum_fusion), kind=kLoop, calls=%fused_computation.12 | loop fusion | flops 6365184 | bytes 8536064 | tf_op jit(solution)/shard_map/add | solution.py:38
  27.9 10.4 %fusion.6 = (f32[256,512]{1,0:T(8,128)}, f32[8,256,512]{2,1,0:T(8,128)}) fusion(f32[8,256,512]{2,1,0:T(8,128)} %param.1, f32[256,512]{1,0:T(8,128)S(1)} %broadcast_multiply_fusion.1, f32[8,256,518]{2,1,0:T(8,128)S(1)} %fusion.5), kind=kLoop, calls=%fused_computation.23 | loop fusion | flops 9306112 | bytes 38797312 | tf_op jit(solution)/shard_map/reduce_sum | solution.py:67
  38.3 0.0 all-gather.3.cloned.1.call-update
  38.3 1.1 slice.141
  39.4 0.6 copy.3
  39.9 1.5 %collective-permute-start.2 = (f32[1,262,512]{2,0,1:T(1,128)S(1)}, f32[1,262,512]{2,0,1:T(1,128)S(1)}, u32[]{:S(2)}, u32[]{:S(2)}) collective-permute-start(f32[1,262,512]{2,0,1:T(1,128)S(1)} %copy.3), channel_id=1, source_target_pairs={{2,0},{4,2},{6,4},{8,6},{10,8},{12,10},{14,12},{3,1},{5,3},{7,5},{... | collective-permute-start | bytes 1609736 | tf_op jit(solution)/shard_map/ppermute | solution.py:29
  41.4 20.9 %collective-permute-done.2 = f32[1,262,512]{2,0,1:T(1,128)S(1)} collective-permute-done((f32[1,262,512]{2,0,1:T(1,128)S(1)}, f32[1,262,512]{2,0,1:T(1,128)S(1)}, u32[]{:S(2)}, u32[]{:S(2)}) %collective-permute-start.2) | collective-permute-done | bytes 536608 | tf_op jit(solution)/shard_map/ppermute | solution.py:29
  62.3 1.4 %fusion.12 = f32[1,256,518]{2,1,0:T(8,128)S(1)} fusion(f32[1,262,512]{2,1,0:T(8,128)S(1)} %copy.4), kind=kLoop, calls=%fused_computation.36 | loop fusion | flops 795648 | bytes 1067008 | tf_op jit(solution)/shard_map/add | solution.py:38
  63.8 55.1 %all-gather.3.cloned.1.call-done = f32[2048,512]{1,0:T(8,128)} async-done(((f32[256,512]{1,0:T(8,128)}), f32[2048,512]{1,0:T(8,128)}) %all-gather.3.cloned.1.call-update) | async-done | bytes 4194320 | tf_op jit(solution)/shard_map/all_gather | solution.py:68
  118.9 2.7 %reduce_sum.19 = f32[256,512]{1,0:T(8,128)S(1)} reduce(f32[8,256,512]{2,1,0:T(8,128)} %bitcast.3, f32[]{:T(128)} %constant.14.clone.1), dimensions={0}, to_apply=%region_1.2 | reduce | flops 917504 | bytes 4718596 | tf_op jit(solution)/shard_map/reduce_sum | solution.py:69
  121.6 3.3 %fusion.41 = (f32[8,256,512]{2,1,0:T(8,128)S(1)}, f32[8,256,512]{2,1,0:T(8,128)S(1)}) fusion(f32[256,512]{1,0:T(8,128)S(1)} %broadcast_multiply_fusion, f32[8,256,512]{2,1,0:T(8,128)} %get-tuple-element.5, f32[256,512]{1,0:T(8,128)S(1)} %broadcast_multiply_fusion.1), kind=kLoop, calls=%fused_computation.88 | loop fusion | flops 2097152 | bytes 13631488 | tf_op jit(solution)/shard_map/log | solution.py:75
  125.0 0.0 copy-start.1
  125.0 0.5 slice.139
  125.5 0.9 fusion.16
  126.5 0.5 copy-done.1
  127.0 3.0 %maximum_subtract_fusion = f32[8,256,512]{2,1,0:T(8,128)} fusion(f32[1,256,512]{2,1,0:T(8,128)S(1)} %fusion.16, f32[7,256,512]{2,1,0:T(8,128)S(1)} %slice.139, f32[8,256,512]{2,1,0:T(8,128)S(1)} %get-tuple-element.3), kind=kLoop, calls=%fused_computation.20 | loop fusion | flops 2097152 | bytes 12582912 | tf_op jit(solution)/shard_map/sub | solution.py:77
  (6 shorter events, 0.1 us)
Async XLA Ops:
  7.2 111.7 %all-gather.3.cloned.1.call-start = ((), (), s32[]{:S(2)}) async-start(), calls=%async_computation | async-start | bytes 4718592 | tf_op jit(solution)/shard_map/all_gather | solution.py:68
  8.2 3.9 %collective-permute-start = (f32[8,3,512]{2,1,0:T(4,128)S(1)}, f32[8,3,512]{2,1,0:T(4,128)S(1)}, u32[]{:S(2)}, u32[]{:S(2)}) collective-permute-start(f32[8,3,512]{2,1,0:T(4,128)S(1)} %get-tuple-element.6), channel_id=1, source_target_pairs={{0,1},{2,3},{4,5},{6,7},{8,9},{10,11},{12,13},{14,15},{16,17},{18,... | collective-permute-start | bytes 147464 | tf_op jit(solution)/shard_map/ppermute | solution.py:17
  10.6 3.1 %collective-permute-start.1 = (f32[8,3,512]{2,1,0:T(4,128)S(1)}, f32[8,3,512]{2,1,0:T(4,128)S(1)}, u32[]{:S(2)}, u32[]{:S(2)}) collective-permute-start(f32[8,3,512]{2,1,0:T(4,128)S(1)} %get-tuple-element.7), channel_id=1, source_target_pairs={{1,0},{3,2},{5,4},{7,6},{9,8},{11,10},{13,12},{15,14},{17,16},{19,... | collective-permute-start | bytes 147464 | tf_op jit(solution)/shard_map/ppermute | solution.py:19
  16.5 11.3 %copy-start = (f32[8,262,512]{2,1,0:T(8,128)}, f32[8,262,512]{2,1,0:T(8,128)S(1)}, u32[]{:S(2)}) copy-start(f32[8,262,512]{2,1,0:T(8,128)S(1)} %pad_maximum_fusion) | copy-start | bytes 12877828
  39.9 22.4 %collective-permute-start.2 = (f32[1,262,512]{2,0,1:T(1,128)S(1)}, f32[1,262,512]{2,0,1:T(1,128)S(1)}, u32[]{:S(2)}, u32[]{:S(2)}) collective-permute-start(f32[1,262,512]{2,0,1:T(1,128)S(1)} %copy.3), channel_id=1, source_target_pairs={{2,0},{4,2},{6,4},{8,6},{10,8},{12,10},{14,12},{3,1},{5,3},{7,5},{... | collective-permute-start | bytes 1609736 | tf_op jit(solution)/shard_map/ppermute | solution.py:29
  125.0 2.0 %copy-start.1 = (f32[8,256,512]{2,1,0:T(8,128)}, f32[8,256,512]{2,1,0:T(8,128)S(1)}, u32[]{:S(2)}) copy-start(f32[8,256,512]{2,1,0:T(8,128)S(1)} %get-tuple-element.3) | copy-start | bytes 12582916
Sparse Core Ops, SparseCore 0:
  38.4 80.4 all-gather.2
